TPU v7x, 256 devices: a whole 4x4x8 slice. The times are simulated.
256 devices in a mesh: seq: 64 (over y, z, core), head: 4 (over x).
Axes of the slice: x: 4, y: 4, z: 8, core: 2. Of those that a mesh axis runs over, the one named last changes fastest.
Arguments:
- queries: bfloat16 [32768, 2048], P('seq', 'head'), may hold values from -6 to 6
- keys: bfloat16 [32768, 2048], P('seq', 'head'), may hold values from -6 to 6
- values: bfloat16 [32768, 2048], P('seq', 'head'), may hold values from -6 to 6
- out_grad: bfloat16 [32768, 4096], P('seq', 'head'), may hold values from -16 to 16
- out_weight: bfloat16 [4096, 2048], P(None, 'head'), may hold values from -0.125 to 0.125
Outputs:
- query_grad: bfloat16 [32768, 2048], P('seq', 'head')
- key_grad: bfloat16 [32768, 2048], P('seq', 'head')
- value_grad: bfloat16 [32768, 2048], P('seq', 'head')
- weight_grad: float32 [4096, 2048], P('seq', 'head')
All inputs are finite; a program needn't handle non-finite values.
Results may differ from a plain program's by a relative error of at most 0.0058.
Values may be sent and summed in bfloat16 or wider, within the bound.
A program may use at most 128 MiB of HBM per device.

v0:
```python
import math
import jax
import jax.numpy as jnp
from jax import lax
from jax.sharding import PartitionSpec as P

HD = 128


def prefix(shard, axis, combine, identity):
    length, mine = (lax.axis_size(axis), lax.axis_index(axis))
    everything = lax.all_gather(shard, axis)
    start = jnp.broadcast_to(jnp.asarray(identity, shard.dtype), shard.shape)

    def turn(k, before):
        at = length - 1 - k
        reached = at > mine
        new = combine(before, everything[at])
        return jnp.where(reached, new, before)

    return lax.fori_loop(0, length, turn, start)


def add_states(earlier, later_part):
    return earlier + later_part


def per_device(queries, keys, values, out_grad, out_weight):
    rows = queries.shape[0]
    local_heads = queries.shape[1] // HD
    total = lax.axis_size("seq") * rows
    scale = 1.0 / math.sqrt(HD * total)
    full_grad = lax.all_gather(out_grad, "head", axis=1, tiled=True)
    attn_grad = jnp.dot(full_grad, out_weight, preferred_element_type=jnp.float32).astype(
        jnp.bfloat16
    )
    shape = (rows, local_heads, HD)
    query = queries.reshape(shape)
    key = keys.reshape(shape)
    value = values.reshape(shape)
    dout = attn_grad.reshape(shape)
    kv_term = scale * jnp.einsum("tha,thb->hab", key, value, preferred_element_type=jnp.float32)
    back_term = scale * jnp.einsum("tha,thb->hab", query, dout, preferred_element_type=jnp.float32)
    zeros = jnp.zeros_like(kv_term)
    position = lax.axis_index("seq")
    piece = lax.all_gather(kv_term[None], "seq", axis=0, tiled=True)
    index = jnp.arange(piece.shape[0], dtype=jnp.int32)
    keep = (index < position).astype(jnp.float32)
    prior_sum = jnp.sum(piece * keep[:, None, None, None], axis=0)
    later_sum = prefix(back_term, "seq", add_states, zeros)
    prior = prior_sum.astype(jnp.bfloat16)
    later = later_sum.astype(jnp.bfloat16)
    mask = jnp.tril(jnp.ones((rows, rows), jnp.float32))
    probs = (
        scale * jnp.einsum("tha,sha->hts", query, key, preferred_element_type=jnp.float32) * mask
    ).astype(jnp.bfloat16)
    grads = (
        scale * jnp.einsum("thb,shb->hts", dout, value, preferred_element_type=jnp.float32) * mask
    ).astype(jnp.bfloat16)
    outputs = (
        jnp.einsum("hts,shb->thb", probs, value, preferred_element_type=jnp.float32)
        + jnp.einsum("tha,hab->thb", query, prior, preferred_element_type=jnp.float32)
    ).astype(jnp.bfloat16)
    query_grad = (
        jnp.einsum("hts,sha->tha", grads, key, preferred_element_type=jnp.float32)
        + jnp.einsum("thb,hab->tha", dout, prior, preferred_element_type=jnp.float32)
    ).astype(jnp.bfloat16)
    key_grad = (
        jnp.einsum("hts,tha->sha", grads, query, preferred_element_type=jnp.float32)
        + jnp.einsum("shb,hab->sha", value, later, preferred_element_type=jnp.float32)
    ).astype(jnp.bfloat16)
    value_grad = (
        jnp.einsum("hts,thb->shb", probs, dout, preferred_element_type=jnp.float32)
        + jnp.einsum("sha,hab->shb", key, later, preferred_element_type=jnp.float32)
    ).astype(jnp.bfloat16)
    flat_out = outputs.reshape(rows, local_heads * HD)
    factor = 1.0 / math.sqrt(total)
    product = lax.dot_general(
        full_grad, flat_out, (((0,), (0,)), ((), ())), preferred_element_type=jnp.float32
    )
    weight_grad = lax.psum_scatter(product * factor, "seq", scatter_dimension=0, tiled=True)
    flat = (rows, local_heads * HD)
    return (query_grad.reshape(flat), key_grad.reshape(flat), value_grad.reshape(flat), weight_grad)


def solution(mesh):
    return jax.shard_map(
        per_device,
        mesh=mesh,
        in_specs=(
            P("seq", "head"),
            P("seq", "head"),
            P("seq", "head"),
            P("seq", "head"),
            P(None, "head"),
        ),
        out_specs=(P("seq", "head"), P("seq", "head"), P("seq", "head"), P("seq", "head")),
        check_vma=False,
    )
```

profile of v0, /device:TPU:2, one launch (start us, length us, event | category | flops | bytes accessed | tf_op | source)
XLA Modules:
  0.0 426.9 jit_solution(13473758385437747828)
XLA Ops:
  8.0 1.3 copy.57
  9.2 2.1 convolution_multiply_fusion.1
  11.4 51.5 %all-gather.6.cloned.1.call-done = bf16[512,4096]{1,0:T(8,128)(2,1)} async-done(((bf16[512,1024]{1,0:T(8,128)(2,1)}), bf16[512,4096]{1,0:T(8,128)(2,1)}) %all-gather.6.cloned.1.call-update) | async-done | bytes 4194320 | tf_op jit(solution)/shard_map/all_gather | solution.py:33
  62.9 5.8 %convolution_convert_fusion = bf16[512,512]{0,1:T(8,128)(2,1)S(1)} fusion(bf16[512,4096]{1,0:T(8,128)(2,1)} %all-gather.6.cloned.1.call-done, bf16[4096,512]{1,0:T(8,128)(2,1)} %param.11), kind=kOutput, calls=%fused_computation.15 | convolution fusion | flops 2147745792 | bytes 8912896 | tf_op jit(solution)/shard_map/dot_general | solution.py:34
  71.0 1.8 convolution_bitcast_fusion.1
  73.5 1.5 convolution_bitcast_fusion
  75.0 1.8 convolution_bitcast_fusion.2
  77.3 89.2 %all-gather.8.cloned.1.call-done = f32[256,128,128]{2,1,0:T(8,128)} async-done(((f32[4,128,128]{2,1,0:T(8,128)}), f32[256,128,128]{2,1,0:T(8,128)}) %all-gather.8.cloned.1.call-update) | async-done | bytes 16777232 | tf_op jit(solution)/shard_map/all_gather | solution.py:46
  166.5 7.7 %multiply_reduce_fusion = bf16[4,128,128]{2,1,0:T(8,128)(2,1)S(1)} fusion(f32[64,4,128,128]{3,2,1,0:T(8,128)} %bitcast.105, f32[64]{0:T(128)S(1)} %compare_convert_fusion), kind=kLoop, calls=%fused_computation.1 | loop fusion | flops 8323072 | bytes 16908544 | tf_op jit(solution)/shard_map/reduce_sum | solution.py:49
  174.3 1.1 fusion.3
  175.4 2.0 copy.47
  177.4 1.6 fusion.6
  179.0 8.0 %multiply_bitcast_fusion = f32[4096,512]{0,1:T(8,128)} fusion(bf16[512,512]{0,1:T(8,128)(2,1)S(1)} %bitcast.114, bf16[512,4096]{1,0:T(8,128)(2,1)} %all-gather.6.cloned.1.call-done), kind=kOutput, calls=%fused_computation.2 | convolution fusion | flops 2149580800 | bytes 13107200 | tf_op jit(solution)/shard_map/dot_general | solution.py:78
  187.0 9.0 %copy.55 = f32[4096,512]{1,0:T(8,128)} copy(f32[4096,512]{0,1:T(8,128)} %multiply_bitcast_fusion) | data formatting | bytes 16777216
  196.0 70.1 %all-gather.10.cloned.1.call-done = f32[256,128,128]{2,1,0:T(8,128)} async-done(((f32[4,128,128]{2,1,0:T(8,128)}), f32[256,128,128]{2,1,0:T(8,128)}) %all-gather.10.cloned.1.call-update) | async-done | bytes 16777232 | tf_op jit(solution)/shard_map/all_gather | solution.py:12
  266.1 68.7 %while.16 = (s32[]{:T(128)}, f32[4,128,128]{2,1,0:T(8,128)S(1)}, s32[]{:T(128)}, f32[64,4,128,128]{3,2,1,0:T(8,128)}, s32[]{:T(128)}, /*index=5*/s32[]{:T(128)}, s32[]{:T(128)}, s32[]{:T(128)}) while((s32[]{:T(128)}, f32[4,128,128]{2,1,0:T(8,128)S(1)}, s32[]{:T(128)}, f32[64,4,128,128]{3,2,1,0:T(8,128)}, s32[]{:T(128)}, ...), condition=%wide.region_2.3_spmd.clone, body=%wide.region_1.2_spmd.clone.sunk | while | flops 196616 | bytes 786595 | solution.py:21
  277.9 1.1 add_select_fusion.2
  288.6 1.1 add_select_fusion.2
  290.8 1.1 add_select_fusion.2
  293.0 1.1 add_select_fusion.2
  311.3 1.1 add_select_fusion.2
  313.4 1.1 add_select_fusion.2
  334.9 1.5 fusion.4
  338.8 81.6 %reduce-scatter.4.cloned.1.call-done = f32[64,512]{1,0:T(8,128)} async-done(((f32[4096,512]{1,0:T(8,128)}), f32[64,512]{1,0:T(8,128)}) %reduce-scatter.4.cloned.1.call-update) | async-done | bytes 131088
  (83 shorter events, 67.2 us)
Async XLA Ops:
  7.2 61.6 %copy-start = (bf16[512,512]{1,0:T(8,128)(2,1)S(1)}, bf16[512,512]{1,0:T(8,128)(2,1)}, u32[]{:S(2)}) copy-start(bf16[512,512]{1,0:T(8,128)(2,1)} %param.7) | copy-start | bytes 1572868
  7.2 55.7 %all-gather.6.cloned.1.call-start = ((), (), s32[]{:S(2)}) async-start(), calls=%async_computation.1 | async-start | bytes 5242880 | tf_op jit(solution)/shard_map/all_gather | solution.py:33
  7.9 158.6 %all-gather.8.cloned.1.call-start = ((), (), s32[]{:S(2)}) async-start(), calls=%async_computation.2 | async-start | bytes 17039360 | tf_op jit(solution)/shard_map/all_gather | solution.py:46
  11.3 58.9 %copy-start.1 = (bf16[512,512]{1,0:T(8,128)(2,1)S(1)}, bf16[512,512]{1,0:T(8,128)(2,1)}, u32[]{:S(2)}) copy-start(bf16[512,512]{1,0:T(8,128)(2,1)} %param.8) | copy-start | bytes 1572868
  11.4 254.8 %all-gather.10.cloned.1.call-start = ((), (), s32[]{:S(2)}) async-start(), calls=%async_computation.3 | async-start | bytes 17039360 | tf_op jit(solution)/shard_map/all_gather | solution.py:12
  69.9 350.4 %reduce-scatter.4.cloned.1.call-start = ((), (), s32[]{:S(2)}) async-start(), calls=%async_computation.4 | async-start | bytes 8519680
  166.5 7.8 %copy-start.2 = (f32[512,4,128]{0,2,1:T(8,128)S(1)}, f32[512,4,128]{0,2,1:T(8,128)}, u32[]{:S(2)}) copy-start(f32[512,4,128]{0,2,1:T(8,128)} %convolution_bitcast_fusion.2) | copy-start | bytes 3145732
Sparse Core Ops, SparseCore 0:
  9.8 53.0 all-gather.5
  66.2 100.2 all-gather.7
  169.9 96.2 all-gather.9
  270.8 149.5 reduce-scatter.3
where the time goes:
time: 429 us; the launch traced here: 427 us
  waiting for transfers between devices  293 us (68%)
  other arithmetic  74.8 us (17%)
  matrix products  27.7 us (6%)
  local copies, waits for them, and re-layouts  15.2 us (4%)
  between operations  13.9 us (3%)
    all_gather x1, waiting for transfers between devices, per_device(): piece = lax.all_gather(kv_term[None], 'seq', axis=0, tiled=True)  89.2 us
    unnamed x5, waiting for transfers between devices  82.3 us
    all_gather x1, waiting for transfers between devices, prefix(): everything = lax.all_gather(shard, axis)  70.1 us
    select_n x64, other arithmetic, turn(): return jnp.where(reached, new, before)  67 us
    all_gather x1, waiting for transfers between devices, per_device(): full_grad = lax.all_gather(out_grad, 'head', axis=1, tiled=True)  51.5 us
    unnamed x10, local copies, waits for them, and re-layouts  13.1 us
  transfers between devices with their start and end apart: 4, of which 4 were waited for; matrix products, arithmetic and copies ran while one was open for 28% of the time, Pallas kernels for 0%

commit v1 on v0

--- a/solution.py
+++ b/solution.py
@@ -30,7 +30,23 @@
     local_heads = queries.shape[1] // HD
     total = lax.axis_size("seq") * rows
     scale = 1.0 / math.sqrt(HD * total)
-    full_grad = lax.all_gather(out_grad, "head", axis=1, tiled=True)
+    ways, here, step = (lax.axis_size("head"), lax.axis_index("head"), out_grad.shape[1])
+    lengths = [n * ways if d == 1 else n for d, n in enumerate(out_grad.shape)]
+    full = lax.dynamic_update_slice_in_dim(
+        jnp.zeros(lengths, out_grad.dtype), out_grad, here * step, axis=1
+    )
+    going_up = going_down = out_grad
+    for far in range(1, ways // 2 + 1):
+        going_up = lax.ppermute(going_up, "head", [(d, (d + 1) % ways) for d in range(ways)])
+        full = lax.dynamic_update_slice_in_dim(full, going_up, (here - far) % ways * step, axis=1)
+        if 2 * far < ways:
+            going_down = lax.ppermute(
+                going_down, "head", [(d, (d - 1) % ways) for d in range(ways)]
+            )
+            full = lax.dynamic_update_slice_in_dim(
+                full, going_down, (here + far) % ways * step, axis=1
+            )
+    full_grad = full
     attn_grad = jnp.dot(full_grad, out_weight, preferred_element_type=jnp.float32).astype(
         jnp.bfloat16
     )

time: 429 us -> 376 us (0.88)
  waiting for transfers between devices: 293 us -> 245 us
  local copies, waits for them, and re-layouts: 15.2 us -> 9.87 us
    unnamed x5 -> x3, waiting for transfers between devices: 82.3 us -> 0.05 us
    reduce_scatter x0 -> x1, waiting for transfers between devices: none -> 81.6 us  [per_device(): lax.psum_scatter(product * factor, 'seq', scatter_dimension=0, tiled=True)]
    all_gather x1 -> x0, waiting for transfers between devices: 51.5 us -> none  [per_device(): full_grad = lax.all_gather(out_grad, 'head', axis=1, tiled=True)]
    all_gather x1, waiting for transfers between devices: 89.2 us -> 41.3 us  [per_device(): piece = lax.all_gather(kv_term[None], 'seq', axis=0, tiled=True)]
    ppermute x0 -> x3, waiting for transfers between devices: none -> 43 us  [the longest x2 43 us: per_device(): lax.ppermute(going_up, 'head', [(d, (d + 1) % ways) for d in range(ways)])]
    all_gather x1, waiting for transfers between devices: 70.1 us -> 79.2 us  [prefix(): everything = lax.all_gather(shard, axis)]
    unnamed x10 -> x15, local copies, waits for them, and re-layouts: 13.1 us -> 4.09 us
  transfers between devices with their start and end apart: 4 -> 6, of which waited for: 4 -> 5; matrix products, arithmetic and copies ran while one was open for 28% -> 28% of each run, Pallas kernels for 0% -> 0%
where the time goes in v1:
time: 376 us; the launch traced here: 374 us
  waiting for transfers between devices  245 us (65%)
  other arithmetic  74.8 us (20%)
  matrix products  24.2 us (6%)
  between operations  14 us (4%)
  local copies, waits for them, and re-layouts  9.87 us (3%)
  starting transfers between devices  4.2 us (1%)
    reduce_scatter x1, waiting for transfers between devices, per_device(): lax.psum_scatter(product * factor, 'seq', scatter_dimension=0, tiled=True)  81.6 us
    all_gather x1, waiting for transfers between devices, prefix(): everything = lax.all_gather(shard, axis)  79.2 us
    select_n x64, other arithmetic, turn(): return jnp.where(reached, new, before)  67 us
    ppermute x2, waiting for transfers between devices, per_device(): lax.ppermute(going_up, 'head', [(d, (d + 1) % ways) for d in range(ways)])  43 us
    all_gather x1, waiting for transfers between devices, per_device(): piece = lax.all_gather(kv_term[None], 'seq', axis=0, tiled=True)  41.3 us
    dot_general x1, matrix products, per_device(): lax.dot_general(full_grad, flat_out, (((0,), (0,)), ((), ())), preferred_...  7.96 us
    reduce_sum x1, other arithmetic, per_device(): prior_sum = jnp.sum(piece * keep[:, None, None, None], axis=0)  7.74 us
  transfers between devices with their start and end apart: 6, of which 5 were waited for; matrix products, arithmetic and copies ran while one was open for 28% of the time, Pallas kernels for 0%

profile of v1, /device:TPU:2, one launch (start us, length us, event | category | flops | bytes accessed | tf_op | source)
XLA Modules:
  0.0 374.1 jit_solution(11269373991708345745)
XLA Ops:
  7.2 1.4 copy.53
  8.6 2.1 convolution_multiply_fusion.2
  10.8 1.6 collective-permute-start
  13.2 22.8 %collective-permute-done = bf16[512,1024]{1,0:T(8,128)(2,1)S(1)} collective-permute-done((bf16[512,1024]{1,0:T(8,128)(2,1)}, bf16[512,1024]{1,0:T(8,128)(2,1)S(1)}, u32[]{:S(2)}, u32[]{:S(2)}) %collective-permute-start) | collective-permute-done | bytes 1048608 | tf_op jit(solution)/shard_map/ppermute | solution.py:40
  36.0 1.5 collective-permute-start.2
  38.2 1.5 constant_dynamic-update-slice_fusion.1
  39.8 20.2 %collective-permute-done.2 = bf16[512,1024]{1,0:T(8,128)(2,1)} collective-permute-done((bf16[512,1024]{1,0:T(8,128)(2,1)S(1)}, bf16[512,1024]{1,0:T(8,128)(2,1)}, u32[]{:S(2)}, u32[]{:S(2)}) %collective-permute-start.2) | collective-permute-done | bytes 1048608 | tf_op jit(solution)/shard_map/ppermute | solution.py:40
  60.0 1.3 constant_dynamic-update-slice_fusion
  61.4 2.4 convolution_convert_fusion
  66.0 1.7 convolution_bitcast_fusion.1
  67.8 1.4 fusion.28
  70.5 1.8 convolution_bitcast_fusion.2
  72.3 41.3 %all-gather.5.cloned.1.call-done = f32[256,128,128]{2,1,0:T(8,128)} async-done(((f32[4,128,128]{2,1,0:T(8,128)}), f32[256,128,128]{2,1,0:T(8,128)}) %all-gather.5.cloned.1.call-update) | async-done | bytes 16777232 | tf_op jit(solution)/shard_map/all_gather | solution.py:62
  113.6 7.7 %multiply_reduce_fusion = bf16[4,128,128]{2,1,0:T(8,128)(2,1)S(1)} fusion(f32[64,4,128,128]{3,2,1,0:T(8,128)} %bitcast.102, f32[64]{0:T(128)S(1)} %compare_convert_fusion), kind=kLoop, calls=%fused_computation.1 | loop fusion | flops 8323072 | bytes 16908544 | tf_op jit(solution)/shard_map/reduce_sum | solution.py:65
  121.3 1.1 fusion.3
  122.4 2.0 copy.46
  124.5 1.6 fusion.6
  126.0 8.0 %convolution_multiply_fusion = f32[4096,512]{1,0:T(8,128)} fusion(bf16[512,4096]{1,0:T(8,128)(2,1)} %copy-done.1, bf16[512,512]{0,1:T(8,128)(2,1)S(1)} %bitcast.111), kind=kOutput, calls=%fused_computation.2 | convolution fusion | flops 2149580800 | bytes 13107200 | tf_op jit(solution)/shard_map/dot_general | solution.py:94
  134.0 79.2 %all-gather.7.cloned.1.call-done = f32[256,128,128]{2,1,0:T(8,128)} async-done(((f32[4,128,128]{2,1,0:T(8,128)}), f32[256,128,128]{2,1,0:T(8,128)}) %all-gather.7.cloned.1.call-update) | async-done | bytes 16777232 | tf_op jit(solution)/shard_map/all_gather | solution.py:12
  213.2 68.9 %while.16 = (s32[]{:T(128)}, f32[4,128,128]{2,1,0:T(8,128)S(1)}, s32[]{:T(128)}, f32[64,4,128,128]{3,2,1,0:T(8,128)}, s32[]{:T(128)}, /*index=5*/s32[]{:T(128)}, s32[]{:T(128)}, s32[]{:T(128)}) while((s32[]{:T(128)}, f32[4,128,128]{2,1,0:T(8,128)S(1)}, s32[]{:T(128)}, f32[64,4,128,128]{3,2,1,0:T(8,128)}, s32[]{:T(128)}, ...), condition=%wide.region_2.3_spmd.clone, body=%wide.region_1.2_spmd.clone.sunk | while | flops 196616 | bytes 786587 | solution.py:21
  225.0 1.1 add_select_fusion.2
  228.2 1.1 add_select_fusion.2
  282.1 1.6 fusion.5
  285.9 81.6 %reduce-scatter.2.cloned.1.call-done = f32[64,512]{1,0:T(8,128)} async-done(((f32[4096,512]{1,0:T(8,128)}), f32[64,512]{1,0:T(8,128)}) %reduce-scatter.2.cloned.1.call-update) | async-done | bytes 131088 | tf_op jit(solution)/shard_map/reduce_scatter | solution.py:97
  (96 shorter events, 72.3 us)
Async XLA Ops:
  7.2 56.6 %copy-start = (bf16[512,512]{1,0:T(8,128)(2,1)S(1)}, bf16[512,512]{1,0:T(8,128)(2,1)}, u32[]{:S(2)}) copy-start(bf16[512,512]{1,0:T(8,128)(2,1)} %param.7) | copy-start | bytes 1572868
  7.2 30.8 %copy-start.4 = (bf16[512,1024]{1,0:T(8,128)(2,1)S(1)}, bf16[512,1024]{1,0:T(8,128)(2,1)}, u32[]{:S(2)}) copy-start(bf16[512,1024]{1,0:T(8,128)(2,1)} %param.10) | copy-start | bytes 3145732
  7.2 106.4 %all-gather.5.cloned.1.call-start = ((), (), s32[]{:S(2)}) async-start(), calls=%async_computation.2 | async-start | bytes 17039360 | tf_op jit(solution)/shard_map/all_gather | solution.py:62
  10.7 202.5 %all-gather.7.cloned.1.call-start = ((), (), s32[]{:S(2)}) async-start(), calls=%async_computation.3 | async-start | bytes 17039360 | tf_op jit(solution)/shard_map/all_gather | solution.py:12
  10.8 25.2 %collective-permute-start = (bf16[512,1024]{1,0:T(8,128)(2,1)}, bf16[512,1024]{1,0:T(8,128)(2,1)S(1)}, u32[]{:S(2)}, u32[]{:S(2)}) collective-permute-start(bf16[512,1024]{1,0:T(8,128)(2,1)} %param.10), channel_id=1, source_target_pairs={{0,1},{1,2},{2,3},{3,0},{4,5},{5,6},{6,7},{7,4},{8,9},{9,10},{10,1... | collective-permute-start | bytes 3145736 | tf_op jit(solution)/shard_map/ppermute | solution.py:40
  12.3 25.9 %collective-permute-start.1 = (bf16[512,1024]{1,0:T(8,128)(2,1)}, bf16[512,1024]{1,0:T(8,128)(2,1)}, u32[]{:S(2)}, u32[]{:S(2)}) collective-permute-start(bf16[512,1024]{1,0:T(8,128)(2,1)} %param.10), channel_id=1, source_target_pairs={{0,3},{1,0},{2,1},{3,2},{4,7},{5,4},{6,5},{7,6},{8,11},{9,8},{10,9... | collective-permute-start | bytes 3145736 | tf_op jit(solution)/shard_map/ppermute | solution.py:43
  36.0 24.0 %collective-permute-start.2 = (bf16[512,1024]{1,0:T(8,128)(2,1)S(1)}, bf16[512,1024]{1,0:T(8,128)(2,1)}, u32[]{:S(2)}, u32[]{:S(2)}) collective-permute-start(bf16[512,1024]{1,0:T(8,128)(2,1)S(1)} %collective-permute-done), channel_id=1, source_target_pairs={{0,1},{1,2},{2,3},{3,0},{4,5},{5,6},{6,7},{7,4},{8,9},{9,10},{10,1... | collective-permute-start | bytes 3145736 | tf_op jit(solution)/shard_map/ppermute | solution.py:40
  38.0 23.4 %copy-start.5 = (bf16[4096,512]{1,0:T(8,128)(2,1)S(1)}, bf16[4096,512]{1,0:T(8,128)(2,1)}, u32[]{:S(2)}) copy-start(bf16[4096,512]{1,0:T(8,128)(2,1)} %param.11) | copy-start | bytes 12582916
  61.3 2.4 copy-start.1
  61.4 4.0 %copy-start.2 = (bf16[512,512]{1,0:T(8,128)(2,1)S(1)}, bf16[512,512]{1,0:T(8,128)(2,1)}, u32[]{:S(2)}) copy-start(bf16[512,512]{1,0:T(8,128)(2,1)} %param.8) | copy-start | bytes 1572868
  64.9 302.6 %reduce-scatter.2.cloned.1.call-start = ((), (), s32[]{:S(2)}) async-start(), calls=%async_computation.1 | async-start | bytes 8519680 | tf_op jit(solution)/shard_map/reduce_scatter | solution.py:97
  113.6 7.8 %copy-start.3 = (f32[512,4,128]{0,2,1:T(8,128)S(1)}, f32[512,4,128]{0,2,1:T(8,128)}, u32[]{:S(2)}) copy-start(f32[512,4,128]{0,2,1:T(8,128)} %convolution_bitcast_fusion.2) | copy-start | bytes 3145732
Sparse Core Ops, SparseCore 0:
  11.3 102.1 all-gather.4
  116.9 96.2 all-gather.6
  218.0 149.5 reduce-scatter.1
